TPU v7x, 32 devices: a whole 2x2x4 slice. The times are simulated.
32 devices in a mesh: ctx: 8 (over y, x, core), page: 4 (over z).
Axes of the slice: x: 2, y: 2, z: 4, core: 2. Of those that a mesh axis runs over, the one named last changes fastest.
Arguments:
- queries: bfloat16 [2048, 8192], P('ctx', 'page'), may hold values from -200 to 200
- keys: bfloat16 [2048, 512], P('ctx', 'page'), may hold values from -6 to 6
- values: bfloat16 [2048, 512], P('ctx', 'page'), may hold values from -6 to 6
- span_table: int32 [16], replicated, may hold values from 0 to 15, each once
- page_slots: int32 [16], replicated, may hold values from 0 to 15, each once
Outputs:
- attended: bfloat16 [2048, 8192], P('ctx', 'page')
- cache_pages: bfloat16 [16, 4, 2, 128, 128], P('ctx')
- cache_scales: float32 [16, 4, 2], P('ctx')
Inputs may be any that keep to these rules, and one draw needn't show every extreme that they name: Stored span i (rows i * 128 to (i + 1) * 128 - 1) holds prompt positions span_table[i] * 128 onward; every value appears once. `page_slots`: every slot is named by exactly one page.
All inputs are finite; a program needn't handle non-finite values. Where the computation divides by a largest or mean magnitude, that divisor is 1e-20 or more.
Results may differ from a plain program's by a relative error of at most 0.0055.
Values may be sent and summed in bfloat16 or wider, within the bound.
A program may use at most 64 MiB of HBM per device.

v0:
```python
import math
import jax
import jax.numpy as jnp
from jax import lax
from jax.sharding import PartitionSpec as P

DH = 128
PAGE = 128
SPAN = 128


def on_device(queries, keys, values, span_table, page_slots):
    rows = queries.shape[0]
    kv_here = keys.shape[1] // DH
    q_here = queries.shape[1] // DH
    group = q_here // kv_here
    ctx_index = lax.axis_index("ctx")
    table_size = span_table.shape[0]
    scale = DH ** (-0.5)

    def token_positions(start, count):
        span_ids = start // SPAN + jnp.arange(count // SPAN, dtype=jnp.int32)
        onehot = span_ids[:, None] == jnp.arange(table_size, dtype=jnp.int32)[None, :]
        placed = jnp.sum(jnp.where(onehot, span_table[None, :], 0), axis=1)
        inner = jnp.arange(SPAN, dtype=jnp.int32)
        return (placed[:, None] * SPAN + inner[None, :]).reshape(count)

    query_pos = token_positions(ctx_index * rows, rows)
    query_heads = queries.reshape(rows, kv_here, group, DH)
    slots_here = rows // PAGE
    first_slot = ctx_index * slots_here
    page_ids = jnp.arange(page_slots.shape[0], dtype=jnp.int32)
    wanted = [
        jnp.sum(jnp.where(page_slots == first_slot + j, page_ids, 0)) for j in range(slots_here)
    ]

    def collect(held, piece):
        count = piece.shape[0]
        updated = []
        for j in range(slots_here):
            offset = wanted[j] * PAGE
            inside = (offset >= 0) & (offset + PAGE <= count)
            clamped = jnp.clip(offset, 0, count - PAGE)
            picked = lax.dynamic_slice_in_dim(piece, clamped, PAGE, 0)
            updated.append(jnp.where(inside, picked, held[j]))
        return jnp.stack(updated, axis=0)

    start_state = (
        jnp.full((kv_here, group, rows), -1e30, jnp.float32),
        jnp.zeros((kv_here, group, rows), jnp.float32),
        jnp.zeros((kv_here, group, rows, DH), jnp.float32),
    )
    empty_pages = jnp.zeros((slots_here, PAGE, kv_here * DH), jnp.bfloat16)
    state = start_state
    key_pages = empty_pages
    value_pages = empty_pages
    key_piece = lax.all_gather(keys, "ctx", axis=0, tiled=True)
    value_piece = lax.all_gather(values, "ctx", axis=0, tiled=True)
    count = key_piece.shape[0]
    key_pos = token_positions(jnp.int32(0), count)
    attend_state = state
    attend_key_piece = key_piece.reshape(count, kv_here, DH)
    attend_value_piece = value_piece.reshape(count, kv_here, DH)
    attend_count = attend_key_piece.shape[0]
    width = math.gcd(attend_count, 512)
    blocks = attend_count // width
    key_blocks = attend_key_piece.reshape(blocks, width, kv_here, DH)
    value_blocks = attend_value_piece.reshape(blocks, width, kv_here, DH)
    pos_blocks = key_pos.reshape(blocks, width)

    def step(carry, block):
        top, total, summed = carry
        key_block, value_block, pos_block = block
        score = (
            jnp.einsum("qhgd,khd->hgqk", query_heads, key_block, preferred_element_type=jnp.float32)
            * scale
        )
        keep = pos_block[None, :] <= query_pos[:, None]
        score = jnp.where(keep[None, None], score, -1e30)
        new_top = jnp.maximum(top, jnp.max(score, axis=-1))
        factor = jnp.exp(top - new_top)
        weight = jnp.where(keep[None, None], jnp.exp(score - new_top[..., None]), 0.0)
        total = total * factor + jnp.sum(weight, axis=-1)
        update = jnp.einsum(
            "hgqk,khd->hgqd",
            weight.astype(jnp.bfloat16),
            value_block,
            preferred_element_type=jnp.float32,
        )
        summed = summed * factor[..., None] + update
        return ((new_top, total, summed), None)

    attend_state, unused = lax.scan(step, attend_state, (key_blocks, value_blocks, pos_blocks))
    state = attend_state
    state, key_pages, value_pages = (
        state,
        collect(key_pages, key_piece),
        collect(value_pages, value_piece),
    )
    key_pages = key_pages.reshape(slots_here, PAGE, kv_here, DH).transpose(0, 2, 1, 3)
    value_pages = value_pages.reshape(slots_here, PAGE, kv_here, DH).transpose(0, 2, 1, 3)
    local_raw = jnp.stack([key_pages, value_pages], axis=2)
    raw = lax.all_gather(local_raw, "page", axis=1, tiled=True)
    top, total, summed = state
    result = summed / total[..., None]
    attended = jnp.transpose(result, (2, 0, 1, 3)).reshape(rows, q_here * DH).astype(jnp.bfloat16)
    raw_float = raw.astype(jnp.float32)
    cache_scales = jnp.max(jnp.abs(raw_float), axis=(3, 4)) + 1e-06
    cache_pages = (raw_float / cache_scales[..., None, None]).astype(jnp.bfloat16)
    return (attended, cache_pages, cache_scales)


def solution(mesh):
    placed = (P("ctx", "page"), P("ctx", "page"), P("ctx", "page"), P(), P())
    return jax.shard_map(
        on_device,
        mesh=mesh,
        in_specs=placed,
        out_specs=(P("ctx", "page"), P("ctx", None, None, None, None), P("ctx", None, None)),
        check_vma=False,
    )
```

profile of v0, /device:TPU:0, one launch (start us, length us, event | category | flops | bytes accessed | tf_op | source)
XLA Modules:
  0.0 111.6 jit_solution(16091338165210521844)
XLA Ops:
  0.7 0.8 select_reduce_fusion
  1.4 0.1 mul.56
  1.5 0.1 broadcast_bitcast_fusion
  1.6 11.6 %all_gather.9 = bf16[2048,128]{1,0:T(8,128)(2,1)S(1)} all-gather(bf16[256,128]{1,0:T(8,128)(2,1)} %param.8), channel_id=1, replica_groups=mesh['ctx'=8,'page'=4] {'ctx'}, dimensions={0}, use_global_device_ids=true | all-gather | bytes 589824 | tf_op jit(solution)/shard_map/all_gather | solution.py:57
  13.2 1.5 %copy.31 = bf16[256,2048]{0,1:T(8,128)(2,1)S(1)} copy(bf16[256,2048]{1,0:T(8,128)(2,1)} %param.7) | data formatting | bytes 2097152 | tf_op args[0]
  14.7 0.7 copy.33
  15.4 9.5 %all_gather.10 = bf16[2048,128]{1,0:T(8,128)(2,1)S(1)} all-gather(bf16[256,128]{1,0:T(8,128)(2,1)} %param.9), channel_id=1, replica_groups=mesh['ctx'=8,'page'=4] {'ctx'}, dimensions={0}, use_global_device_ids=true | all-gather | bytes 589824 | tf_op jit(solution)/shard_map/all_gather | solution.py:58
  24.9 0.8 fusion.26
  25.8 0.0 copy-start.1
  25.8 61.7 %while.15 = (s32[]{:T(128)}, f32[1,16,256]{2,1,0:T(8,128)S(1)}, f32[1,16,256]{2,1,0:T(8,128)S(1)}, f32[1,16,256,128]{3,2,1,0:T(8,128)}, s32[4,512]{1,0:T(4,128)S...) while((s32[]{:T(128)}, f32[1,16,256]{2,1,0:T(8,128)S(1)}, ...), condition=%wide.region_5.6_spmd.clone, body=%wide.region_2.5_spmd.clone.sunk | while | flops 1102733568 | bytes 65020080 | solution.py:93
  25.8 0.1 add_bitcast_fusion.2
  25.9 0.1 broadcast_compare_fusion.2
  26.0 4.6 %fusion.36 = (f32[16,256]{1,0:T(8,128)S(1)}, f32[512,256,16]{1,0,2:T(8,128)}) fusion(pred[256,512]{0,1:T(8,128)(4,1)S(1)} %broadcast_compare_fusion.2, bf16[256,1,16,128]{3,0,2,1:T(8,128)(2,1)S(1)} %get-tuple-element.249, bf16[4,512,1,128]{3,1,2,0:T(8,128)(2,1)S(1)} %get-tuple-element.248, s32[]{:T(128)S(6)} %copy.48), kind=kOutput, calls=%fused_computation.3.clone.1 | convolution fusion | flops 543158272 | bytes 9715716 | tf_op jit(solution)/shard_map/while/body/eval_jaxpr/qhgd,khd->hgqk/dot_general | solution.py:75
  30.6 0.0 copy-start
  30.6 4.6 %fusion.38 = f32[16,256]{1,0:T(8,128)S(1)} fusion(f32[512,256,16]{1,0,2:T(8,128)} %get-tuple-element.219, f32[16,256]{1,0:T(8,128)S(1)} %bitcast.114, pred[256,512]{0,1:T(8,128)(4,1)S(1)} %broadcast_compare_fusion.2), kind=kLoop, calls=%fused_computation.5.clone.1 | loop fusion | flops 10481664 | bytes 8552448 | tf_op jit(solution)/shard_map/while/body/eval_jaxpr/reduce_sum | solution.py:83
  35.2 1.2 %copy-done = f32[512,256,16]{1,0,2:T(8,128)S(1)} copy-done((f32[512,256,16]{1,0,2:T(8,128)S(1)}, f32[512,256,16]{1,0,2:T(8,128)}, u32[]{:S(2)}) %copy-start) | copy-done | bytes 8388632 | tf_op jit(solution)/shard_map/while
  36.4 3.9 %bitcast_add_fusion.6 = f32[1,16,256,128]{3,2,1,0:T(8,128)} fusion(f32[1,16,256,128]{3,2,1,0:T(8,128)} %get-tuple-element.235, f32[512,256,16]{1,0,2:T(8,128)S(1)} %copy-done, f32[16,256]{1,0:T(8,128)S(1)} %bitcast.115, pred[256,512]{0,1:T(8,128)(4,1)S(1)} %broadcast_compare_fusion.2, f32[16,256]{1,0:T(8,128)S(1)} %get-tuple-element.220, ...), kind=kOutput, calls=%fused_computation.9.clone.1 | convolution fusion | flops 548929536 | bytes 12877829 | tf_op jit(solution)/shard_map/while/body/eval_jaxpr/hgqk,khd->hgqd/dot_general | solution.py:84
  40.3 0.1 add_bitcast_fusion.2
  40.4 0.1 broadcast_compare_fusion.2
  40.5 4.6 %fusion.36 = (f32[16,256]{1,0:T(8,128)S(1)}, f32[512,256,16]{1,0,2:T(8,128)}) fusion(pred[256,512]{0,1:T(8,128)(4,1)S(1)} %broadcast_compare_fusion.2, bf16[256,1,16,128]{3,0,2,1:T(8,128)(2,1)S(1)} %get-tuple-element.249, bf16[4,512,1,128]{3,1,2,0:T(8,128)(2,1)S(1)} %get-tuple-element.248, s32[]{:T(128)S(6)} %copy.48), kind=kOutput, calls=%fused_computation.3.clone.1 | convolution fusion | flops 543158272 | bytes 9715716 | tf_op jit(solution)/shard_map/while/body/eval_jaxpr/qhgd,khd->hgqk/dot_general | solution.py:75
  45.1 0.0 copy-start
  45.1 4.6 %fusion.38 = f32[16,256]{1,0:T(8,128)S(1)} fusion(f32[512,256,16]{1,0,2:T(8,128)} %get-tuple-element.219, f32[16,256]{1,0:T(8,128)S(1)} %bitcast.114, pred[256,512]{0,1:T(8,128)(4,1)S(1)} %broadcast_compare_fusion.2), kind=kLoop, calls=%fused_computation.5.clone.1 | loop fusion | flops 10481664 | bytes 8552448 | tf_op jit(solution)/shard_map/while/body/eval_jaxpr/reduce_sum | solution.py:83
  49.7 1.2 %copy-done = f32[512,256,16]{1,0,2:T(8,128)S(1)} copy-done((f32[512,256,16]{1,0,2:T(8,128)S(1)}, f32[512,256,16]{1,0,2:T(8,128)}, u32[]{:S(2)}) %copy-start) | copy-done | bytes 8388632 | tf_op jit(solution)/shard_map/while
  50.9 5.1 %bitcast_add_fusion.6 = f32[1,16,256,128]{3,2,1,0:T(8,128)} fusion(f32[1,16,256,128]{3,2,1,0:T(8,128)} %get-tuple-element.235, f32[512,256,16]{1,0,2:T(8,128)S(1)} %copy-done, f32[16,256]{1,0:T(8,128)S(1)} %bitcast.115, pred[256,512]{0,1:T(8,128)(4,1)S(1)} %broadcast_compare_fusion.2, f32[16,256]{1,0:T(8,128)S(1)} %get-tuple-element.220, ...), kind=kOutput, calls=%fused_computation.9.clone.1 | convolution fusion | flops 548929536 | bytes 12877829 | tf_op jit(solution)/shard_map/while/body/eval_jaxpr/hgqk,khd->hgqd/dot_general | solution.py:84
  56.0 0.1 add_bitcast_fusion.2
  56.1 0.1 broadcast_compare_fusion.2
  56.2 4.6 %fusion.36 = (f32[16,256]{1,0:T(8,128)S(1)}, f32[512,256,16]{1,0,2:T(8,128)}) fusion(pred[256,512]{0,1:T(8,128)(4,1)S(1)} %broadcast_compare_fusion.2, bf16[256,1,16,128]{3,0,2,1:T(8,128)(2,1)S(1)} %get-tuple-element.249, bf16[4,512,1,128]{3,1,2,0:T(8,128)(2,1)S(1)} %get-tuple-element.248, s32[]{:T(128)S(6)} %copy.48), kind=kOutput, calls=%fused_computation.3.clone.1 | convolution fusion | flops 543158272 | bytes 9715716 | tf_op jit(solution)/shard_map/while/body/eval_jaxpr/qhgd,khd->hgqk/dot_general | solution.py:75
  60.8 0.0 copy-start
  60.8 4.6 %fusion.38 = f32[16,256]{1,0:T(8,128)S(1)} fusion(f32[512,256,16]{1,0,2:T(8,128)} %get-tuple-element.219, f32[16,256]{1,0:T(8,128)S(1)} %bitcast.114, pred[256,512]{0,1:T(8,128)(4,1)S(1)} %broadcast_compare_fusion.2), kind=kLoop, calls=%fused_computation.5.clone.1 | loop fusion | flops 10481664 | bytes 8552448 | tf_op jit(solution)/shard_map/while/body/eval_jaxpr/reduce_sum | solution.py:83
  65.5 1.2 %copy-done = f32[512,256,16]{1,0,2:T(8,128)S(1)} copy-done((f32[512,256,16]{1,0,2:T(8,128)S(1)}, f32[512,256,16]{1,0,2:T(8,128)}, u32[]{:S(2)}) %copy-start) | copy-done | bytes 8388632 | tf_op jit(solution)/shard_map/while
  66.6 5.1 %bitcast_add_fusion.6 = f32[1,16,256,128]{3,2,1,0:T(8,128)} fusion(f32[1,16,256,128]{3,2,1,0:T(8,128)} %get-tuple-element.235, f32[512,256,16]{1,0,2:T(8,128)S(1)} %copy-done, f32[16,256]{1,0:T(8,128)S(1)} %bitcast.115, pred[256,512]{0,1:T(8,128)(4,1)S(1)} %broadcast_compare_fusion.2, f32[16,256]{1,0:T(8,128)S(1)} %get-tuple-element.220, ...), kind=kOutput, calls=%fused_computation.9.clone.1 | convolution fusion | flops 548929536 | bytes 12877829 | tf_op jit(solution)/shard_map/while/body/eval_jaxpr/hgqk,khd->hgqd/dot_general | solution.py:84
  71.7 0.1 add_bitcast_fusion.2
  71.8 0.1 broadcast_compare_fusion.2
  72.0 4.6 %fusion.36 = (f32[16,256]{1,0:T(8,128)S(1)}, f32[512,256,16]{1,0,2:T(8,128)}) fusion(pred[256,512]{0,1:T(8,128)(4,1)S(1)} %broadcast_compare_fusion.2, bf16[256,1,16,128]{3,0,2,1:T(8,128)(2,1)S(1)} %get-tuple-element.249, bf16[4,512,1,128]{3,1,2,0:T(8,128)(2,1)S(1)} %get-tuple-element.248, s32[]{:T(128)S(6)} %copy.48), kind=kOutput, calls=%fused_computation.3.clone.1 | convolution fusion | flops 543158272 | bytes 9715716 | tf_op jit(solution)/shard_map/while/body/eval_jaxpr/qhgd,khd->hgqk/dot_general | solution.py:75
  76.5 0.0 copy-start
  76.5 4.6 %fusion.38 = f32[16,256]{1,0:T(8,128)S(1)} fusion(f32[512,256,16]{1,0,2:T(8,128)} %get-tuple-element.219, f32[16,256]{1,0:T(8,128)S(1)} %bitcast.114, pred[256,512]{0,1:T(8,128)(4,1)S(1)} %broadcast_compare_fusion.2), kind=kLoop, calls=%fused_computation.5.clone.1 | loop fusion | flops 10481664 | bytes 8552448 | tf_op jit(solution)/shard_map/while/body/eval_jaxpr/reduce_sum | solution.py:83
  81.2 1.2 %copy-done = f32[512,256,16]{1,0,2:T(8,128)S(1)} copy-done((f32[512,256,16]{1,0,2:T(8,128)S(1)}, f32[512,256,16]{1,0,2:T(8,128)}, u32[]{:S(2)}) %copy-start) | copy-done | bytes 8388632 | tf_op jit(solution)/shard_map/while
  82.4 5.1 %bitcast_add_fusion.6 = f32[1,16,256,128]{3,2,1,0:T(8,128)} fusion(f32[1,16,256,128]{3,2,1,0:T(8,128)} %get-tuple-element.235, f32[512,256,16]{1,0,2:T(8,128)S(1)} %copy-done, f32[16,256]{1,0:T(8,128)S(1)} %bitcast.115, pred[256,512]{0,1:T(8,128)(4,1)S(1)} %broadcast_compare_fusion.2, f32[16,256]{1,0:T(8,128)S(1)} %get-tuple-element.220, ...), kind=kOutput, calls=%fused_computation.9.clone.1 | convolution fusion | flops 548929536 | bytes 12877829 | tf_op jit(solution)/shard_map/while/body/eval_jaxpr/hgqk,khd->hgqd/dot_general | solution.py:84
  87.5 1.9 %fusion.25 = bf16[256,1,16,128]{3,0,2,1:T(8,128)(2,1)S(1)} fusion(f32[1,16,256,128]{3,2,1,0:T(8,128)} %get-tuple-element.51, f32[16,256]{1,0:T(8,128)S(1)} %bitcast.123), kind=kLoop, calls=%fused_computation.36 | loop fusion | flops 1048576 | bytes 3162112 | tf_op jit(solution)/shard_map/convert_element_type | solution.py:106
  89.4 0.7 copy.35
  90.1 1.2 %copy.43 = bf16[32,8,16,128]{3,1,2,0:T(8,128)(2,1)} copy(bf16[32,8,16,128]{3,2,1,0:T(8,128)(2,1)S(1)} %bitcast.116) | data formatting | bytes 2097152
  91.3 0.0 copy-done.1
  91.3 0.6 fusion.27
  93.3 0.1 select_bitcast_fusion.1
  93.4 16.3 %all_gather.11 = bf16[2,4,2,128,128]{4,3,2,1,0:T(8,128)(2,1)S(1)} all-gather(bf16[2,1,2,128,128]{4,3,2,1,0:T(8,128)(2,1)S(1)} %pad_maximum_fusion), channel_id=1, replica_groups=mesh['ctx'=8,'page'=4] {'page'}, dimensions={1}, use_global_device_ids=true | all-gather | bytes 655360 | tf_op jit(solution)/shard_map/all_gather | solution.py:103
  109.8 0.2 fusion.23
  110.0 1.0 fusion.24
  111.0 0.7 copy.37
  (28 shorter events, 0.2 us)
Async XLA Ops:
  25.8 65.6 %copy-start.1 = (s32[16]{0:T(128)S(1)}, s32[16]{0:T(128)}, u32[]{:S(2)}) copy-start(s32[16]{0:T(128)} %param.11) | copy-start | bytes 196
  30.6 5.8 %copy-start = (f32[512,256,16]{1,0,2:T(8,128)S(1)}, f32[512,256,16]{1,0,2:T(8,128)}, u32[]{:S(2)}) copy-start(f32[512,256,16]{1,0,2:T(8,128)} %get-tuple-element.219) | copy-start | bytes 25165828 | tf_op jit(solution)/shard_map/while
  45.1 5.8 %copy-start = (f32[512,256,16]{1,0,2:T(8,128)S(1)}, f32[512,256,16]{1,0,2:T(8,128)}, u32[]{:S(2)}) copy-start(f32[512,256,16]{1,0,2:T(8,128)} %get-tuple-element.219) | copy-start | bytes 25165828 | tf_op jit(solution)/shard_map/while
  60.8 5.8 %copy-start = (f32[512,256,16]{1,0,2:T(8,128)S(1)}, f32[512,256,16]{1,0,2:T(8,128)}, u32[]{:S(2)}) copy-start(f32[512,256,16]{1,0,2:T(8,128)} %get-tuple-element.219) | copy-start | bytes 25165828 | tf_op jit(solution)/shard_map/while
  76.5 5.8 %copy-start = (f32[512,256,16]{1,0,2:T(8,128)S(1)}, f32[512,256,16]{1,0,2:T(8,128)}, u32[]{:S(2)}) copy-start(f32[512,256,16]{1,0,2:T(8,128)} %get-tuple-element.219) | copy-start | bytes 25165828 | tf_op jit(solution)/shard_map/while
where the time goes:
time: 112 us
  blocking collectives  37.5 us (33%)
  matrix products  37.4 us (33%)
  other arithmetic  24.8 us (22%)
  local copies, waits for them, and re-layouts  9.68 us (9%)
  between operations  2.05 us (2%)
    dot_general x4, matrix products, step(): jnp.einsum('hgqk,khd->hgqd', weight.astype(jnp.bfloat16), value_block, pr...  19.1 us
    reduce_sum x4, other arithmetic, step(): total = total * factor + jnp.sum(weight, axis=-1)  18.4 us
    dot_general x4, matrix products, step(): jnp.einsum('qhgd,khd->hgqk', query_heads, key_block, preferred_element_ty...  18.3 us
    all_gather x1, blocking collectives, on_device(): raw = lax.all_gather(local_raw, 'page', axis=1, tiled=True)  16.3 us
    all_gather x1, blocking collectives, on_device(): key_piece = lax.all_gather(keys, 'ctx', axis=0, tiled=True)  11.6 us
    all_gather x1, blocking collectives, on_device(): value_piece = lax.all_gather(values, 'ctx', axis=0, tiled=True)  9.53 us
    while x12, local copies, waits for them, and re-layouts  4.76 us
    unnamed x7, local copies, waits for them, and re-layouts  4.13 us

commit v1 on v0

--- a/solution.py
+++ b/solution.py
@@ -54,8 +54,11 @@
     state = start_state
     key_pages = empty_pages
     value_pages = empty_pages
-    key_piece = lax.all_gather(keys, "ctx", axis=0, tiled=True)
-    value_piece = lax.all_gather(values, "ctx", axis=0, tiled=True)
+    key_piece, value_piece = jnp.split(
+        lax.all_gather(jnp.concatenate([keys, values], axis=1), "ctx", axis=0, tiled=True),
+        [keys.shape[1]],
+        axis=1,
+    )
     count = key_piece.shape[0]
     key_pos = token_positions(jnp.int32(0), count)
     attend_state = state

time: 112 us -> 129 us (1.15)
  blocking collectives: 37.5 us -> 16 us
  waiting for transfers between devices: 0 us -> 21 us
  between operations: 2.05 us -> 15.5 us
  other arithmetic: 24.8 us -> 27.1 us
    all_gather x2 -> x0, blocking collectives: 21.2 us -> none  [the longest x1 11.6 us: on_device(): key_piece = lax.all_gather(keys, 'ctx', axis=0, tiled=True)]
    all_gather x0 -> x1, waiting for transfers between devices: none -> 21 us  [on_device(): lax.all_gather(jnp.concatenate([keys, values], axis=1), 'ctx', axis=0, ti...]
    concatenate x0 -> x1, other arithmetic: none -> 1.54 us  [on_device(): jnp.concatenate([keys, values], axis=1)]
    unnamed x7 -> x5, local copies, waits for them, and re-layouts: 4.13 us -> 4.13 us
  transfers between devices with their start and end apart: 0 -> 1, of which waited for: 0 -> 1; matrix products, arithmetic and copies ran while one was open for 0% -> 4% of each run, Pallas kernels for 0% -> 0%
where the time goes in v1:
time: 129 us; the launch traced here: 128 us
  matrix products  37.4 us (29%)
  other arithmetic  27.1 us (21%)
  waiting for transfers between devices  21 us (16%)
  blocking collectives  16 us (12%)
  between operations  15.5 us (12%)
  local copies, waits for them, and re-layouts  10.9 us (8%)
    all_gather x1, waiting for transfers between devices, on_device(): lax.all_gather(jnp.concatenate([keys, values], axis=1), 'ctx', axis=0, ti...  21 us
    dot_general x4, matrix products, step(): jnp.einsum('hgqk,khd->hgqd', weight.astype(jnp.bfloat16), value_block, pr...  19.1 us
    reduce_sum x4, other arithmetic, step(): total = total * factor + jnp.sum(weight, axis=-1)  18.4 us
    dot_general x4, matrix products, step(): jnp.einsum('qhgd,khd->hgqk', query_heads, key_block, preferred_element_ty...  18.3 us
    all_gather x1, blocking collectives, on_device(): raw = lax.all_gather(local_raw, 'page', axis=1, tiled=True)  16 us
    while x12, local copies, waits for them, and re-layouts  4.76 us
    unnamed x5, local copies, waits for them, and re-layouts  4.13 us
  transfers between devices with their start and end apart: 1, of which 1 were waited for; matrix products, arithmetic and copies ran while one was open for 4% of the time, Pallas kernels for 0%

profile of v1, /device:TPU:0, one launch (start us, length us, event | category | flops | bytes accessed | tf_op | source)
XLA Modules:
  0.0 128.2 jit_solution(9111311375720837800)
XLA Ops:
  7.2 0.0 all-gather.2.cloned.1.call-start
  7.2 1.5 %pad_maximum_fusion = bf16[256,256]{1,0:T(8,128)(2,1)} fusion(bf16[256,128]{1,0:T(8,128)(2,1)} %param.9, bf16[256,128]{1,0:T(8,128)(2,1)} %param.8), kind=kLoop, calls=%fused_computation.37 | loop fusion | flops 262144 | bytes 262144 | tf_op jit(solution)/shard_map/concatenate | solution.py:58
  8.8 0.0 all-gather.2.cloned.1.call-update
  8.8 1.4 %fusion.27 = (s32[]{:T(128)}, s32[]{:T(128)}) fusion(s32[16]{0:T(128)} %param.11, s32[]{:T(128)S(6)} %mul.59, s32[]{:T(128)S(6)} %add.91), kind=kLoop, calls=%fused_computation.55 | loop fusion | flops 94 | bytes 80 | tf_op jit(solution)/shard_map/reduce_sum | solution.py:34
  11.5 0.8 select_reduce_fusion
  12.3 0.1 mul.56
  12.4 1.5 %copy.31 = bf16[256,2048]{0,1:T(8,128)(2,1)S(1)} copy(bf16[256,2048]{1,0:T(8,128)(2,1)} %param.7) | data formatting | bytes 2097152 | tf_op args[0]
  13.9 0.7 copy.33
  14.6 0.8 fusion.26
  15.5 0.1 broadcast_bitcast_fusion
  15.6 21.0 %all-gather.2.cloned.1.call-done = bf16[2048,256]{1,0:T(8,128)(2,1)} async-done(((bf16[256,256]{1,0:T(8,128)(2,1)}), bf16[2048,256]{1,0:T(8,128)(2,1)}) %all-gather.2.cloned.1.call-update) | async-done | bytes 1048592 | tf_op jit(solution)/shard_map/all_gather | solution.py:58
  36.6 1.3 fusion.29
  37.8 0.1 select_bitcast_fusion.1
  38.0 16.0 %all_gather.7 = bf16[2,4,2,128,128]{4,3,2,1,0:T(8,128)(2,1)S(1)} all-gather(bf16[2,1,2,128,128]{4,3,2,1,0:T(8,128)(2,1)S(1)} %pad_maximum_fusion.1), channel_id=1, replica_groups=mesh['ctx'=8,'page'=4] {'page'}, dimensions={1}, use_global_device_ids=true | all-gather | bytes 655360 | tf_op jit(solution)/shard_map/all_gather | solution.py:106
  54.0 0.2 fusion.23
  54.2 1.0 fusion.24
  55.2 0.7 copy.37
  55.8 61.7 %while.15 = (s32[]{:T(128)}, f32[1,16,256]{2,1,0:T(8,128)S(1)}, f32[1,16,256]{2,1,0:T(8,128)S(1)}, f32[1,16,256,128]{3,2,1,0:T(8,128)}, s32[4,512]{1,0:T(4,128)S...) while((s32[]{:T(128)}, f32[1,16,256]{2,1,0:T(8,128)S(1)}, ...), condition=%wide.region_5.6_spmd.clone, body=%wide.region_2.5_spmd.clone.sunk | while | flops 1102733568 | bytes 65020080 | solution.py:96
  55.8 0.1 add_bitcast_fusion.2
  55.9 0.1 broadcast_compare_fusion.2
  56.1 4.6 %fusion.37 = (f32[16,256]{1,0:T(8,128)S(1)}, f32[512,256,16]{1,0,2:T(8,128)}) fusion(pred[256,512]{0,1:T(8,128)(4,1)S(1)} %broadcast_compare_fusion.2, bf16[256,1,16,128]{3,0,2,1:T(8,128)(2,1)S(1)} %get-tuple-element.251, bf16[4,512,1,128]{3,1,2,0:T(8,128)(2,1)S(1)} %get-tuple-element.250, s32[]{:T(128)S(6)} %copy.48), kind=kOutput, calls=%fused_computation.3.clone.1 | convolution fusion | flops 543158272 | bytes 9715716 | tf_op jit(solution)/shard_map/while/body/eval_jaxpr/qhgd,khd->hgqk/dot_general | solution.py:78
  60.6 0.0 copy-start
  60.7 4.6 %fusion.39 = f32[16,256]{1,0:T(8,128)S(1)} fusion(f32[512,256,16]{1,0,2:T(8,128)} %get-tuple-element.221, f32[16,256]{1,0:T(8,128)S(1)} %bitcast.114, pred[256,512]{0,1:T(8,128)(4,1)S(1)} %broadcast_compare_fusion.2), kind=kLoop, calls=%fused_computation.5.clone.1 | loop fusion | flops 10481664 | bytes 8552448 | tf_op jit(solution)/shard_map/while/body/eval_jaxpr/reduce_sum | solution.py:86
  65.3 1.2 copy-done
  66.5 3.9 %bitcast_add_fusion.6 = f32[1,16,256,128]{3,2,1,0:T(8,128)} fusion(f32[1,16,256,128]{3,2,1,0:T(8,128)} %get-tuple-element.237, f32[512,256,16]{1,0,2:T(8,128)S(1)} %copy-done, f32[16,256]{1,0:T(8,128)S(1)} %bitcast.115, pred[256,512]{0,1:T(8,128)(4,1)S(1)} %broadcast_compare_fusion.2, f32[16,256]{1,0:T(8,128)S(1)} %get-tuple-element.222, ...), kind=kOutput, calls=%fused_computation.9.clone.1 | convolution fusion | flops 548929536 | bytes 12877829 | tf_op jit(solution)/shard_map/while/body/eval_jaxpr/hgqk,khd->hgqd/dot_general | solution.py:87
  70.3 0.1 add_bitcast_fusion.2
  70.4 0.1 broadcast_compare_fusion.2
  70.6 4.6 %fusion.37 = (f32[16,256]{1,0:T(8,128)S(1)}, f32[512,256,16]{1,0,2:T(8,128)}) fusion(pred[256,512]{0,1:T(8,128)(4,1)S(1)} %broadcast_compare_fusion.2, bf16[256,1,16,128]{3,0,2,1:T(8,128)(2,1)S(1)} %get-tuple-element.251, bf16[4,512,1,128]{3,1,2,0:T(8,128)(2,1)S(1)} %get-tuple-element.250, s32[]{:T(128)S(6)} %copy.48), kind=kOutput, calls=%fused_computation.3.clone.1 | convolution fusion | flops 543158272 | bytes 9715716 | tf_op jit(solution)/shard_map/while/body/eval_jaxpr/qhgd,khd->hgqk/dot_general | solution.py:78
  75.1 0.0 copy-start
  75.2 4.6 %fusion.39 = f32[16,256]{1,0:T(8,128)S(1)} fusion(f32[512,256,16]{1,0,2:T(8,128)} %get-tuple-element.221, f32[16,256]{1,0:T(8,128)S(1)} %bitcast.114, pred[256,512]{0,1:T(8,128)(4,1)S(1)} %broadcast_compare_fusion.2), kind=kLoop, calls=%fused_computation.5.clone.1 | loop fusion | flops 10481664 | bytes 8552448 | tf_op jit(solution)/shard_map/while/body/eval_jaxpr/reduce_sum | solution.py:86
  79.8 1.2 copy-done
  81.0 5.1 %bitcast_add_fusion.6 = f32[1,16,256,128]{3,2,1,0:T(8,128)} fusion(f32[1,16,256,128]{3,2,1,0:T(8,128)} %get-tuple-element.237, f32[512,256,16]{1,0,2:T(8,128)S(1)} %copy-done, f32[16,256]{1,0:T(8,128)S(1)} %bitcast.115, pred[256,512]{0,1:T(8,128)(4,1)S(1)} %broadcast_compare_fusion.2, f32[16,256]{1,0:T(8,128)S(1)} %get-tuple-element.222, ...), kind=kOutput, calls=%fused_computation.9.clone.1 | convolution fusion | flops 548929536 | bytes 12877829 | tf_op jit(solution)/shard_map/while/body/eval_jaxpr/hgqk,khd->hgqd/dot_general | solution.py:87
  86.1 0.1 add_bitcast_fusion.2
  86.1 0.1 broadcast_compare_fusion.2
  86.3 4.6 %fusion.37 = (f32[16,256]{1,0:T(8,128)S(1)}, f32[512,256,16]{1,0,2:T(8,128)}) fusion(pred[256,512]{0,1:T(8,128)(4,1)S(1)} %broadcast_compare_fusion.2, bf16[256,1,16,128]{3,0,2,1:T(8,128)(2,1)S(1)} %get-tuple-element.251, bf16[4,512,1,128]{3,1,2,0:T(8,128)(2,1)S(1)} %get-tuple-element.250, s32[]{:T(128)S(6)} %copy.48), kind=kOutput, calls=%fused_computation.3.clone.1 | convolution fusion | flops 543158272 | bytes 9715716 | tf_op jit(solution)/shard_map/while/body/eval_jaxpr/qhgd,khd->hgqk/dot_general | solution.py:78
  90.9 0.0 copy-start
  90.9 4.6 %fusion.39 = f32[16,256]{1,0:T(8,128)S(1)} fusion(f32[512,256,16]{1,0,2:T(8,128)} %get-tuple-element.221, f32[16,256]{1,0:T(8,128)S(1)} %bitcast.114, pred[256,512]{0,1:T(8,128)(4,1)S(1)} %broadcast_compare_fusion.2), kind=kLoop, calls=%fused_computation.5.clone.1 | loop fusion | flops 10481664 | bytes 8552448 | tf_op jit(solution)/shard_map/while/body/eval_jaxpr/reduce_sum | solution.py:86
  95.5 1.2 copy-done
  96.7 5.1 %bitcast_add_fusion.6 = f32[1,16,256,128]{3,2,1,0:T(8,128)} fusion(f32[1,16,256,128]{3,2,1,0:T(8,128)} %get-tuple-element.237, f32[512,256,16]{1,0,2:T(8,128)S(1)} %copy-done, f32[16,256]{1,0:T(8,128)S(1)} %bitcast.115, pred[256,512]{0,1:T(8,128)(4,1)S(1)} %broadcast_compare_fusion.2, f32[16,256]{1,0:T(8,128)S(1)} %get-tuple-element.222, ...), kind=kOutput, calls=%fused_computation.9.clone.1 | convolution fusion | flops 548929536 | bytes 12877829 | tf_op jit(solution)/shard_map/while/body/eval_jaxpr/hgqk,khd->hgqd/dot_general | solution.py:87
  101.8 0.1 add_bitcast_fusion.2
  101.9 0.1 broadcast_compare_fusion.2
  102.0 4.6 %fusion.37 = (f32[16,256]{1,0:T(8,128)S(1)}, f32[512,256,16]{1,0,2:T(8,128)}) fusion(pred[256,512]{0,1:T(8,128)(4,1)S(1)} %broadcast_compare_fusion.2, bf16[256,1,16,128]{3,0,2,1:T(8,128)(2,1)S(1)} %get-tuple-element.251, bf16[4,512,1,128]{3,1,2,0:T(8,128)(2,1)S(1)} %get-tuple-element.250, s32[]{:T(128)S(6)} %copy.48), kind=kOutput, calls=%fused_computation.3.clone.1 | convolution fusion | flops 543158272 | bytes 9715716 | tf_op jit(solution)/shard_map/while/body/eval_jaxpr/qhgd,khd->hgqk/dot_general | solution.py:78
  106.6 0.0 copy-start
  106.6 4.6 %fusion.39 = f32[16,256]{1,0:T(8,128)S(1)} fusion(f32[512,256,16]{1,0,2:T(8,128)} %get-tuple-element.221, f32[16,256]{1,0:T(8,128)S(1)} %bitcast.114, pred[256,512]{0,1:T(8,128)(4,1)S(1)} %broadcast_compare_fusion.2), kind=kLoop, calls=%fused_computation.5.clone.1 | loop fusion | flops 10481664 | bytes 8552448 | tf_op jit(solution)/shard_map/while/body/eval_jaxpr/reduce_sum | solution.py:86
  111.2 1.2 copy-done
  112.4 5.1 %bitcast_add_fusion.6 = f32[1,16,256,128]{3,2,1,0:T(8,128)} fusion(f32[1,16,256,128]{3,2,1,0:T(8,128)} %get-tuple-element.237, f32[512,256,16]{1,0,2:T(8,128)S(1)} %copy-done, f32[16,256]{1,0:T(8,128)S(1)} %bitcast.115, pred[256,512]{0,1:T(8,128)(4,1)S(1)} %broadcast_compare_fusion.2, f32[16,256]{1,0:T(8,128)S(1)} %get-tuple-element.222, ...), kind=kOutput, calls=%fused_computation.9.clone.1 | convolution fusion | flops 548929536 | bytes 12877829 | tf_op jit(solution)/shard_map/while/body/eval_jaxpr/hgqk,khd->hgqd/dot_general | solution.py:87
  117.5 1.9 %fusion.25 = bf16[256,1,16,128]{3,0,2,1:T(8,128)(2,1)S(1)} fusion(f32[1,16,256,128]{3,2,1,0:T(8,128)} %get-tuple-element.51, f32[16,256]{1,0:T(8,128)S(1)} %bitcast.121), kind=kLoop, calls=%fused_computation.36 | loop fusion | flops 1048576 | bytes 3162112 | tf_op jit(solution)/shard_map/convert_element_type | solution.py:109
  119.5 0.7 copy.35
  120.1 1.2 copy.43
  (28 shorter events, 0.2 us)
Async XLA Ops:
  7.2 29.4 %all-gather.2.cloned.1.call-start = ((), (), s32[]{:S(2)}) async-start(), calls=%async_computation | async-start | bytes 1179648 | tf_op jit(solution)/shard_map/all_gather | solution.py:58
  60.6 5.8 %copy-start = (f32[512,256,16]{1,0,2:T(8,128)S(1)}, f32[512,256,16]{1,0,2:T(8,128)}, u32[]{:S(2)}) copy-start(f32[512,256,16]{1,0,2:T(8,128)} %get-tuple-element.221) | copy-start | bytes 25165828 | tf_op jit(solution)/shard_map/while
  75.1 5.8 %copy-start = (f32[512,256,16]{1,0,2:T(8,128)S(1)}, f32[512,256,16]{1,0,2:T(8,128)}, u32[]{:S(2)}) copy-start(f32[512,256,16]{1,0,2:T(8,128)} %get-tuple-element.221) | copy-start | bytes 25165828 | tf_op jit(solution)/shard_map/while
  90.9 5.8 %copy-start = (f32[512,256,16]{1,0,2:T(8,128)S(1)}, f32[512,256,16]{1,0,2:T(8,128)}, u32[]{:S(2)}) copy-start(f32[512,256,16]{1,0,2:T(8,128)} %get-tuple-element.221) | copy-start | bytes 25165828 | tf_op jit(solution)/shard_map/while
  106.6 5.8 %copy-start = (f32[512,256,16]{1,0,2:T(8,128)S(1)}, f32[512,256,16]{1,0,2:T(8,128)}, u32[]{:S(2)}) copy-start(f32[512,256,16]{1,0,2:T(8,128)} %get-tuple-element.221) | copy-start | bytes 25165828 | tf_op jit(solution)/shard_map/while
Sparse Core Ops, SparseCore 0:
  10.4 26.0 all-gather.1
